TPU v7x, 32 devices: a whole 2x2x4 slice. The times are simulated.
32 devices in a mesh: row: 8 (over z, x), col: 4 (over y, core).
Axes of the slice: x: 2, y: 2, z: 4, core: 2. Of those that a mesh axis runs over, the one named last changes fastest.
Arguments:
- features: bfloat16 [32768, 1024], P(('row', 'col')), may hold values from -12 to 12
- cotangent: bfloat16 [32768, 1024], P(('row', 'col')), may hold values from -6 to 6
- loader: int32 [32768], replicated, may hold values from 0 to 32767, as said below
- w_query: bfloat16 [1024, 1024], replicated, may hold values from -2 to 2
- w_key: bfloat16 [1024, 1024], replicated, may hold values from -2 to 2
- w_value: bfloat16 [1024, 1024], replicated, may hold values from -0.1875 to 0.1875
- norm_gain: float32 [1024], replicated, may hold values from 0.25 to 1.75
- send_blocks: int32 [32, 4, 2], replicated, may hold values from -1 to 7, as said below
- tile_lists: int32 [256, 3], P(('row', 'col')), may hold values from 0 to 15, as said below
Outputs:
- layer_out: bfloat16 [32768, 1024], P(('row', 'col'))
- grad_features: bfloat16 [32768, 1024], P(('row', 'col'))
Inputs may be any that keep to these rules, and one draw needn't show every extreme that they name: `loader`: a permutation of the 32768 node numbers; the 1024 rows of each device hold exactly 32 nodes owned by each device. `send_blocks`: entry [e, p, s] is a block of device e (a number below 8) sent to the device of e's row group with col index p in slot s, or -1 for an empty slot; the nonempty slots of one (e, p) come first and name distinct blocks; slots toward e's own col index are empty; all 2 slots toward the next col index (cyclically) are filled. `tile_lists`: row b names 3 distinct entries of the tile table of b's device, never b's own block and never an empty slot; every nonempty received slot is named by some block of its device.
All inputs are finite; a program needn't handle non-finite values.
Results may differ from a plain program's by a relative error of at most 0.012.
The roundings to bfloat16 on the way count: a program that leaves them out, or rounds other values in their place, can miss the bound.
Values may be sent and summed in bfloat16 or wider, within the bound.
No kernel may reach another device: no remote copies, remote signals or barrier semaphores. Data moves between devices by JAX's collectives and lax.ppermute only.
A program may use at most 256 MiB of HBM per device.

v0:
```python
import jax
import jax.numpy as jnp
from jax import lax
from jax.sharding import PartitionSpec as P

HEADS = 8
HEAD_DIM = 128


def attend(queries, key_rows, value_rows, cot_rows, gain_row):
    count = queries.shape[0]
    width = queries.shape[2]
    q_heads = queries.reshape(count, -1, HEADS, HEAD_DIM)
    k_heads = key_rows.reshape(count, -1, HEADS, HEAD_DIM)
    v_heads = value_rows.reshape(count, -1, HEADS, HEAD_DIM)
    score_scale = HEAD_DIM ** (-0.5)
    scores = (
        jnp.einsum("bqhd,bkhd->bhqk", q_heads, k_heads, preferred_element_type=jnp.float32)
        * score_scale
    )
    row_max = jnp.max(scores, axis=-1, keepdims=True)
    expo = jnp.exp(scores - row_max)
    prob_full = expo / jnp.sum(expo, axis=-1, keepdims=True)
    prob_half = prob_full.astype(jnp.bfloat16)
    mixed_out = jnp.einsum(
        "bhqk,bkhd->bqhd", prob_half, v_heads, preferred_element_type=jnp.float32
    ).reshape(count, -1, width)
    inv_rms = lax.rsqrt(jnp.mean(mixed_out * mixed_out, axis=-1, keepdims=True) + 1e-06)
    normed = (mixed_out * inv_rms * gain_row).astype(jnp.bfloat16)
    grad_in = cot_rows.astype(jnp.float32) * gain_row
    inner = jnp.mean(grad_in * mixed_out, axis=-1, keepdims=True)
    grad_mix = (inv_rms * (grad_in - mixed_out * inv_rms * inv_rms * inner)).astype(jnp.bfloat16)
    grad_heads = grad_mix.reshape(count, -1, HEADS, HEAD_DIM)
    grad_prob = jnp.einsum(
        "bqhd,bkhd->bhqk", grad_heads, v_heads, preferred_element_type=jnp.float32
    )
    delta = jnp.sum(prob_full * grad_prob, axis=-1, keepdims=True)
    grad_score = (prob_full * (grad_prob - delta) * score_scale).astype(jnp.bfloat16)
    grad_query = jnp.einsum(
        "bhqk,bkhd->bqhd", grad_score, k_heads, preferred_element_type=jnp.float32
    )
    grad_query = grad_query.reshape(count, -1, width).astype(jnp.bfloat16)
    grad_key = jnp.einsum(
        "bhqk,bqhd->bkhd", grad_score, q_heads, preferred_element_type=jnp.float32
    ).reshape(count, -1, width)
    grad_value = jnp.einsum(
        "bhqk,bqhd->bkhd", prob_half, grad_heads, preferred_element_type=jnp.float32
    ).reshape(count, -1, width)
    return (normed, grad_query, grad_key, grad_value)


def project_back(kv_rows, w_key, w_value, width):
    contract = (((1,), (1,)), ((), ()))
    total = lax.dot_general(kv_rows[:, :width], w_key, contract, preferred_element_type=jnp.float32)
    return total + lax.dot_general(
        kv_rows[:, width:], w_value, contract, preferred_element_type=jnp.float32
    )


def body(features, cotangent, loader, w_query, w_key, w_value, norm_gain, send_blocks, tile_lists):
    row_count = lax.axis_size("row")
    col_count = lax.axis_size("col")
    devices = row_count * col_count
    self_index = lax.axis_index("row") * col_count + lax.axis_index("col")
    rows_dev = features.shape[0]
    width = features.shape[1]
    per_peer = rows_dev // devices
    block_count = tile_lists.shape[0]
    block_rows = rows_dev // block_count
    capacity = send_blocks.shape[2]
    slots = block_count + col_count * capacity
    my_nodes = lax.dynamic_slice_in_dim(loader, self_index * rows_dev, rows_dev)
    send_order = jnp.argsort(my_nodes // rows_dev, stable=True)
    back_order = jnp.argsort(send_order)
    all_owners = (loader // rows_dev).reshape(devices, rows_dev)
    arrive_pos = jnp.argsort(jnp.where(all_owners == self_index, 0, 1), axis=1, stable=True)[
        :, :per_peer
    ]
    arriving = (
        jnp.take_along_axis(loader.reshape(devices, rows_dev), arrive_pos, axis=1).reshape(rows_dev)
        - self_index * rows_dev
    )
    placing = jnp.argsort(arriving)

    def regroup(buffer):
        return lax.all_to_all(buffer, ("row", "col"), split_axis=0, concat_axis=0, tiled=True)

    outgoing = jnp.concatenate([features[send_order], cotangent[send_order]], axis=1).reshape(
        devices, per_peer, 2 * width
    )
    incoming = regroup(outgoing).reshape(rows_dev, 2 * width)[placing]
    owned_rows = incoming[:, :width]
    owned_cot = incoming[:, width:]
    queries = jnp.dot(owned_rows, w_query, preferred_element_type=jnp.float32).astype(jnp.bfloat16)
    key_all = jnp.dot(owned_rows, w_key, preferred_element_type=jnp.float32).astype(jnp.bfloat16)
    value_all = jnp.dot(owned_rows, w_value, preferred_element_type=jnp.float32).astype(
        jnp.bfloat16
    )
    kv_local = jnp.concatenate([key_all, value_all], axis=1).reshape(
        block_count, block_rows, 2 * width
    )
    send_row = lax.dynamic_index_in_dim(send_blocks, self_index, 0, keepdims=False)
    filled = (send_row >= 0)[:, :, None, None]
    picked = jnp.maximum(send_row, 0)
    outbound = jnp.where(filled, kv_local[picked], jnp.zeros((), jnp.bfloat16))
    arrived_kv = lax.all_to_all(outbound, "col", split_axis=0, concat_axis=0, tiled=True).reshape(
        col_count * capacity, block_rows, 2 * width
    )
    tile_table = jnp.concatenate([kv_local, arrived_kv], axis=0)
    read_entries = jnp.concatenate(
        [jnp.arange(block_count, dtype=jnp.int32)[:, None], tile_lists], axis=1
    )
    group_size = 4
    group_count = block_count // group_size

    def per_group(totals, inputs):
        q_group, cot_group, read_group = inputs
        picked_kv = tile_table[read_group].reshape(group_size, -1, 2 * width)
        normed, grad_query, grad_key, grad_value = attend(
            q_group, picked_kv[:, :, :width], picked_kv[:, :, width:], cot_group, norm_gain
        )
        grad_tiles = jnp.concatenate(
            [grad_key.reshape(-1, block_rows, width), grad_value.reshape(-1, block_rows, width)],
            axis=2,
        )
        totals = totals.at[read_group.reshape(-1)].add(grad_tiles)
        return (totals, (normed, grad_query))

    group_inputs = (
        queries.reshape(group_count, group_size, block_rows, width),
        owned_cot.reshape(group_count, group_size, block_rows, width),
        read_entries.reshape(group_count, group_size, -1),
    )
    start = jnp.zeros((slots, block_rows, 2 * width), jnp.float32)
    entry_grads, (normed_all, grad_query_all) = lax.scan(per_group, start, group_inputs)
    remote_kv = entry_grads[block_count:].astype(jnp.bfloat16)
    back_hot = (
        send_row[:, :, None] == jnp.arange(block_count, dtype=jnp.int32)[None, None, :]
    ).astype(jnp.float32)
    back_hot = back_hot.reshape(col_count * capacity, block_count)
    remote_rows = remote_kv.reshape(col_count * capacity * block_rows, 2 * width)
    remote_proj = project_back(remote_rows, w_key, w_value, width).astype(jnp.bfloat16)
    remote_proj = remote_proj.reshape(col_count, capacity, block_rows * width)
    returned = lax.all_to_all(remote_proj, "col", split_axis=0, concat_axis=0, tiled=True)
    returned = returned.reshape(col_count * capacity, block_rows * width).astype(jnp.float32)
    back_sum = lax.dot_general(
        back_hot, returned, (((0,), (0,)), ((), ())), precision=lax.Precision.HIGHEST
    )
    local_kv = entry_grads[:block_count].reshape(rows_dev, 2 * width).astype(jnp.bfloat16)
    grad_query_rows = grad_query_all.reshape(rows_dev, width)
    contract = (((1,), (1,)), ((), ()))
    grad_owned = lax.dot_general(
        grad_query_rows, w_query, contract, preferred_element_type=jnp.float32
    )
    grad_owned = grad_owned + project_back(local_kv, w_key, w_value, width)
    grad_owned = (grad_owned + back_sum.reshape(rows_dev, width)).astype(jnp.bfloat16)
    layer_rows = normed_all.reshape(rows_dev, width)
    layer_back = regroup(layer_rows[arriving].reshape(devices, per_peer, width)).reshape(
        rows_dev, width
    )[back_order]
    grad_back = regroup(grad_owned[arriving].reshape(devices, per_peer, width)).reshape(
        rows_dev, width
    )[back_order]
    return (layer_back, grad_back)


def solution(mesh):
    in_specs = (
        P(("row", "col"), None),
        P(("row", "col"), None),
        P(),
        P(),
        P(),
        P(),
        P(),
        P(),
        P(("row", "col"), None),
    )
    out_specs = (P(("row", "col"), None), P(("row", "col"), None))
    return jax.shard_map(body, mesh=mesh, in_specs=in_specs, out_specs=out_specs, check_vma=False)
```

profile of v0, /device:TPU:0, one launch (start us, length us, event | category | flops | bytes accessed | tf_op | source)
XLA Modules:
  0.0 880.2 jit_solution(3138944694689780795)
XLA Ops:
  12.4 7.9 gather_fusion.1
  20.3 7.9 gather_fusion.2
  32.9 7.4 all-to-all-start
  48.6 8.6 gather_fusion.9
  62.4 72.3 %all-to-all-done = bf16[32,32,2048]{2,1,0:T(8,128)(2,1)} async-done(((bf16[32,32,2048]{2,1,0:T(8,128)(2,1)}), bf16[32,32,2048]{2,1,0:T(8,128)(2,1)}, u32[]{:S(2)}, u32[]{:S(2)}) %all-to-all-start) | async-done | bytes 4194336 | tf_op jit(solution)/shard_map/all_to_all | solution.py:86
  134.7 11.6 %gather_fusion.3 = bf16[1024,2048]{1,0:T(8,128)(2,1)} fusion(bf16[1024,2048]{1,0:T(8,128)(2,1)} %bitcast.16, s32[1024]{0:T(1024)S(1)} %fusion.62), kind=kCustom, calls=%fused_computation.3 | custom fusion | bytes 8392704 | tf_op jit(solution)/shard_map/gather | solution.py:91
  155.2 6.5 copy.81
  171.2 20.7 %all-to-all-start.1 = ((bf16[4,2,128,2048]{3,2,1,0:T(8,128)(2,1)}), bf16[4,2,128,2048]{3,2,1,0:T(8,128)(2,1)}, u32[]{:S(2)}, u32[]{:S(2)}) async-start(bf16[4,2,128,2048]{3,2,1,0:T(8,128)(2,1)} %broadcast_select_fusion), calls=%async_computation.1 | async-start | bytes 8388608 | tf_op jit(solution)/shard_map/all_to_all | solution.py:106
  200.5 39.6 %all-to-all-done.1 = bf16[4,2,128,2048]{3,2,1,0:T(8,128)(2,1)} async-done(((bf16[4,2,128,2048]{3,2,1,0:T(8,128)(2,1)}), bf16[4,2,128,2048]{3,2,1,0:T(8,128)(2,1)}, u32[]{:S(2)}, u32[]{:S(2)}) %all-to-all-start.1) | async-done | bytes 4194336 | tf_op jit(solution)/shard_map/all_to_all | solution.py:106
  240.1 7.4 pad_maximum_fusion.1
  247.5 7.8 broadcast_in_dim.30
  255.3 454.2 %while.14 = (s32[]{:T(128)}, f32[16,128,2048]{2,1,0:T(8,128)}, bf16[2,4,128,1024]{3,2,1,0:T(8,128)(2,1)}, bf16[2,4,128,1024]{3,2,1,0:T(8,128)(2,1)}, s32[2,4,4]{...) while((s32[]{:T(128)}, f32[16,128,2048]{2,1,0:T(8,128)}, ...), condition=%wide.region_10.11_spmd, body=%wide.region_3.10_spmd.sunk | while | flops 3283102720 | bytes 372362752 | solution.py:135
  255.4 8.1 gather_fusion
  269.4 6.2 copy.101
  278.2 8.5 fusion.122
  286.7 6.2 copy.99
  295.5 6.5 fusion.123
  309.6 35.2 %fusion.127 = bf16[4,8,128,128]{3,2,1,0:T(8,128)(2,1)} fusion(bf16[4,512,8,128]{1,3,2,0:T(8,128)(2,1)} %bitcast.135, f32[4,8,128,512]{3,2,1,0:T(8,128)} %fusion.125, f32[4,8,128,512]{3,2,1,0:T(8,128)} %get-tuple-element.201, f32[4,8,128]{2,1,0:T(8,128)S(1)} %get-tuple-element.202), kind=kOutput, calls=%fused_computation.43.clone.1 | convolution fusion | flops 552079872 | bytes 22036480 | tf_op jit(solution)/shard_map/while/body/eval_jaxpr/bhqk,bkhd->bqhd/dot_general | solution.py:39
  354.2 35.9 %fusion.126 = f32[4,512,8,128]{1,3,2,0:T(8,128)} fusion(bf16[4,128,8,128]{1,3,2,0:T(8,128)(2,1)} %bitcast.140, f32[4,8,128,512]{3,2,1,0:T(8,128)} %fusion.125, f32[4,8,128,512]{3,2,1,0:T(8,128)} %get-tuple-element.201, f32[4,8,128]{2,1,0:T(8,128)S(1)} %get-tuple-element.202), kind=kOutput, calls=%fused_computation.24.clone.1 | convolution fusion | flops 551555584 | bytes 26230784 | tf_op jit(solution)/shard_map/while/body/eval_jaxpr/bhqk,bqhd->bkhd/dot_general | solution.py:43
  390.1 9.9 %copy.103 = f32[4,512,8,128]{3,2,1,0:T(8,128)} copy(f32[4,512,8,128]{1,3,2,0:T(8,128)} %fusion.126) | data formatting | bytes 16777216 | tf_op jit(solution)/shard_map/while/body/eval_jaxpr/bhqk,bqhd->bkhd/transpose | solution.py:43
  400.0 9.3 %reshape.404 = f32[16,128,1024]{2,1,0:T(8,128)} reshape(f32[4,512,8,128]{3,2,1,0:T(8,128)} %copy.103) | data formatting | bytes 16777216 | tf_op jit(solution)/shard_map/while/body/eval_jaxpr/reshape;while/body/eval_jaxpr/reshape | solution.py:123
  409.4 7.9 convolution_bitcast_fusion.3
  417.3 9.9 %copy.102 = f32[4,512,8,128]{3,2,1,0:T(8,128)} copy(f32[4,512,8,128]{1,3,2,0:T(8,128)} %convolution_bitcast_fusion.3) | data formatting | bytes 16777216 | tf_op jit(solution)/shard_map/while/body/eval_jaxpr/bhqk,bqhd->bkhd/transpose | solution.py:46
  427.2 9.2 %reshape.403 = f32[16,128,1024]{2,1,0:T(8,128)} reshape(f32[4,512,8,128]{3,2,1,0:T(8,128)} %copy.102) | data formatting | bytes 16777216 | tf_op jit(solution)/shard_map/while/body/eval_jaxpr/reshape;while/body/eval_jaxpr/reshape | solution.py:123
  436.4 11.7 %pad_maximum_fusion.5 = f32[16,128,2048]{2,1,0:T(8,128)} fusion(f32[16,128,1024]{2,1,0:T(8,128)} %reshape.403, f32[16,128,1024]{2,1,0:T(8,128)} %reshape.404), kind=kLoop, calls=%fused_computation.13.clone.1 | loop fusion | flops 4194304 | bytes 33554432 | tf_op jit(solution)/shard_map/while/body/eval_jaxpr/concatenate | solution.py:122
  448.2 34.2 %scatter_fusion = f32[16,128,2048]{2,1,0:T(8,128)} fusion(f32[16,128,2048]{2,1,0:T(8,128)} %get-tuple-element.219, s32[16]{0:T(128)S(1)} %fusion.120, f32[16,128,2048]{2,1,0:T(8,128)} %pad_maximum_fusion.5), kind=kCustom, calls=%fused_computation.10.clone.1 | custom fusion | flops 4194304 | bytes 50331712 | tf_op jit(solution)/shard_map/while/body/eval_jaxpr/scatter-add | solution.py:126
  482.5 8.1 gather_fusion
  505.3 8.5 fusion.122
  513.8 6.2 copy.99
  522.6 6.5 fusion.123
  536.7 35.2 %fusion.127 = bf16[4,8,128,128]{3,2,1,0:T(8,128)(2,1)} fusion(bf16[4,512,8,128]{1,3,2,0:T(8,128)(2,1)} %bitcast.135, f32[4,8,128,512]{3,2,1,0:T(8,128)} %fusion.125, f32[4,8,128,512]{3,2,1,0:T(8,128)} %get-tuple-element.201, f32[4,8,128]{2,1,0:T(8,128)S(1)} %get-tuple-element.202), kind=kOutput, calls=%fused_computation.43.clone.1 | convolution fusion | flops 552079872 | bytes 22036480 | tf_op jit(solution)/shard_map/while/body/eval_jaxpr/bhqk,bkhd->bqhd/dot_general | solution.py:39
  581.3 35.9 %fusion.126 = f32[4,512,8,128]{1,3,2,0:T(8,128)} fusion(bf16[4,128,8,128]{1,3,2,0:T(8,128)(2,1)} %bitcast.140, f32[4,8,128,512]{3,2,1,0:T(8,128)} %fusion.125, f32[4,8,128,512]{3,2,1,0:T(8,128)} %get-tuple-element.201, f32[4,8,128]{2,1,0:T(8,128)S(1)} %get-tuple-element.202), kind=kOutput, calls=%fused_computation.24.clone.1 | convolution fusion | flops 551555584 | bytes 26230784 | tf_op jit(solution)/shard_map/while/body/eval_jaxpr/bhqk,bqhd->bkhd/dot_general | solution.py:43
  617.2 9.9 %copy.103 = f32[4,512,8,128]{3,2,1,0:T(8,128)} copy(f32[4,512,8,128]{1,3,2,0:T(8,128)} %fusion.126) | data formatting | bytes 16777216 | tf_op jit(solution)/shard_map/while/body/eval_jaxpr/bhqk,bqhd->bkhd/transpose | solution.py:43
  627.1 9.3 %reshape.404 = f32[16,128,1024]{2,1,0:T(8,128)} reshape(f32[4,512,8,128]{3,2,1,0:T(8,128)} %copy.103) | data formatting | bytes 16777216 | tf_op jit(solution)/shard_map/while/body/eval_jaxpr/reshape;while/body/eval_jaxpr/reshape | solution.py:123
  636.5 7.9 convolution_bitcast_fusion.3
  644.4 9.9 %copy.102 = f32[4,512,8,128]{3,2,1,0:T(8,128)} copy(f32[4,512,8,128]{1,3,2,0:T(8,128)} %convolution_bitcast_fusion.3) | data formatting | bytes 16777216 | tf_op jit(solution)/shard_map/while/body/eval_jaxpr/bhqk,bqhd->bkhd/transpose | solution.py:46
  654.3 9.2 %reshape.403 = f32[16,128,1024]{2,1,0:T(8,128)} reshape(f32[4,512,8,128]{3,2,1,0:T(8,128)} %copy.102) | data formatting | bytes 16777216 | tf_op jit(solution)/shard_map/while/body/eval_jaxpr/reshape;while/body/eval_jaxpr/reshape | solution.py:123
  663.5 11.7 %pad_maximum_fusion.5 = f32[16,128,2048]{2,1,0:T(8,128)} fusion(f32[16,128,1024]{2,1,0:T(8,128)} %reshape.403, f32[16,128,1024]{2,1,0:T(8,128)} %reshape.404), kind=kLoop, calls=%fused_computation.13.clone.1 | loop fusion | flops 4194304 | bytes 33554432 | tf_op jit(solution)/shard_map/while/body/eval_jaxpr/concatenate | solution.py:122
  675.3 34.2 %scatter_fusion = f32[16,128,2048]{2,1,0:T(8,128)} fusion(f32[16,128,2048]{2,1,0:T(8,128)} %get-tuple-element.219, s32[16]{0:T(128)S(1)} %fusion.120, f32[16,128,2048]{2,1,0:T(8,128)} %pad_maximum_fusion.5), kind=kCustom, calls=%fused_computation.10.clone.1 | custom fusion | flops 4194304 | bytes 50331712 | tf_op jit(solution)/shard_map/while/body/eval_jaxpr/scatter-add | solution.py:126
  709.5 6.6 convert.5
  733.8 7.9 gather_fusion.5
  741.7 17.7 %all-to-all-done.3 = bf16[4,2,131072]{2,1,0:T(2,128)(2,1)} async-done(((bf16[4,2,131072]{2,1,0:T(2,128)(2,1)}), bf16[4,2,131072]{2,1,0:T(2,128)(2,1)}, u32[]{:S(2)}, u32[]{:S(2)}) %all-to-all-start.3) | async-done | bytes 2097184 | tf_op jit(solution)/shard_map/all_to_all | solution.py:144
  784.9 9.6 %add_convert_fusion = bf16[1024,1024]{1,0:T(8,128)(2,1)} fusion(f32[1024,1024]{1,0:T(8,128)} %reshape.283, f32[1024,1024]{1,0:T(8,128)} %fusion.48, f32[1024,1024]{1,0:T(8,128)} %fusion.46, bf16[1024,1024]{1,0:T(8,128)(2,1)} %bitcast.159, bf16[1024,1024]{1,0:T(8,128)(2,1)} %param.14), kind=kOutput, calls=%fused_computation.65 | convolution fusion | flops 2151677952 | bytes 18874368 | tf_op jit(solution)/shard_map/dot_general | solution.py:152
  794.4 7.9 gather_fusion.7
  802.3 9.9 %all-to-all-done.2 = bf16[32,32,1024]{2,1,0:T(8,128)(2,1)} async-done(((bf16[32,32,1024]{2,1,0:T(8,128)(2,1)}), bf16[32,32,1024]{2,1,0:T(8,128)(2,1)}, u32[]{:S(2)}, u32[]{:S(2)}) %all-to-all-start.2) | async-done | bytes 2097184 | tf_op jit(solution)/shard_map/all_to_all | solution.py:86
  820.9 7.9 gather_fusion.6
  828.8 36.5 %all-to-all-done.4 = bf16[32,32,1024]{2,1,0:T(8,128)(2,1)} async-done(((bf16[32,32,1024]{2,1,0:T(8,128)(2,1)}), bf16[32,32,1024]{2,1,0:T(8,128)(2,1)}, u32[]{:S(2)}, u32[]{:S(2)}) %all-to-all-start.4) | async-done | bytes 2097184 | tf_op jit(solution)/shard_map/all_to_all | solution.py:86
  865.3 7.9 gather_fusion.8
  (146 shorter events, 164.8 us)
Async XLA Ops:
  7.2 139.1 %copy-start = (bf16[1024,1024]{1,0:T(8,128)(2,1)S(1)}, bf16[1024,1024]{1,0:T(8,128)(2,1)}, u32[]{:S(2)}) copy-start(bf16[1024,1024]{1,0:T(8,128)(2,1)} %param.16) | copy-start | bytes 6291460
  12.4 7.9 copy-start.13
  32.9 7.5 copy-start.9
  32.9 9.0 %copy-start.17 = (s32[32,4,2]{0,2,1:T(2,128)S(1)}, s32[32,4,2]{0,2,1:T(2,128)}, u32[]{:S(2)}) copy-start(s32[32,4,2]{0,2,1:T(2,128)} %param.18) | copy-start | bytes 3076
  32.9 101.8 %all-to-all-start = ((bf16[32,32,2048]{2,1,0:T(8,128)(2,1)}), bf16[32,32,2048]{2,1,0:T(8,128)(2,1)}, u32[]{:S(2)}, u32[]{:S(2)}) async-start(bf16[32,32,2048]{2,1,0:T(8,128)(2,1)} %bitcast.146), calls=%async_computation | async-start | bytes 8388608 | tf_op jit(solution)/shard_map/all_to_all | solution.py:86
  40.3 7.5 sort.70.cloned.1.call-start
  42.2 0.6 copy-start.15
  57.9 88.3 %copy-start.11 = (s32[32,32]{1,0:T(8,128)}, s32[32,32]{1,0:T(8,128)S(1)}, u32[]{:S(2)}) copy-start(s32[32,32]{1,0:T(8,128)S(1)} %select_subtract_fusion) | copy-start | bytes 12292
  146.2 4.1 copy-start.6
  146.2 4.2 copy-start.19
  171.1 20.7 %copy-start.18 = (s32[8,3]{0,1:T(4,128)S(1)}, s32[8,3]{0,1:T(4,128)}, u32[]{:S(2)}) copy-start(s32[8,3]{0,1:T(4,128)} %param.19) | copy-start | bytes 292
  171.2 68.9 %all-to-all-start.1 = ((bf16[4,2,128,2048]{3,2,1,0:T(8,128)(2,1)}), bf16[4,2,128,2048]{3,2,1,0:T(8,128)(2,1)}, u32[]{:S(2)}, u32[]{:S(2)}) async-start(bf16[4,2,128,2048]{3,2,1,0:T(8,128)(2,1)} %broadcast_select_fusion), calls=%async_computation.1 | async-start | bytes 8388608 | tf_op jit(solution)/shard_map/all_to_all | solution.py:106
  192.0 3.3 copy-start.7
  247.5 7.8 copy-start.10
  295.5 7.9 copy-start.3
  302.0 1.4 copy-start.2
  302.0 3.1 copy-start.1
  304.0 1.0 copy-start.4
  400.0 9.3 %copy-start.5 = (bf16[4,128,8,128]{1,3,2,0:T(8,128)(2,1)S(1)}, bf16[4,128,8,128]{1,3,2,0:T(8,128)(2,1)}, u32[]{:S(2)}) copy-start(bf16[4,128,8,128]{1,3,2,0:T(8,128)(2,1)} %copy-done.4) | copy-start | bytes 3145732 | tf_op jit(solution)/shard_map/while
  522.6 7.9 copy-start.3
  529.2 1.4 copy-start.2
  529.2 3.1 copy-start.1
  531.1 1.0 copy-start.4
  627.1 9.3 %copy-start.5 = (bf16[4,128,8,128]{1,3,2,0:T(8,128)(2,1)S(1)}, bf16[4,128,8,128]{1,3,2,0:T(8,128)(2,1)}, u32[]{:S(2)}) copy-start(bf16[4,128,8,128]{1,3,2,0:T(8,128)(2,1)} %copy-done.4) | copy-start | bytes 3145732 | tf_op jit(solution)/shard_map/while
  718.6 2.4 copy-start.20
  724.7 9.0 %copy-start.12 = (s32[32,32]{1,0:T(8,128)S(1)}, s32[32,32]{1,0:T(8,128)}, u32[]{:S(2)}) copy-start(s32[32,32]{1,0:T(8,128)} %copy-done.11) | copy-start | bytes 12292
  729.2 30.3 %all-to-all-start.3 = ((bf16[4,2,131072]{2,1,0:T(2,128)(2,1)}), bf16[4,2,131072]{2,1,0:T(2,128)(2,1)}, u32[]{:S(2)}, u32[]{:S(2)}) async-start(bf16[4,2,131072]{2,1,0:T(2,128)(2,1)} %reshape.282), calls=%async_computation.3 | async-start | bytes 4194304 | tf_op jit(solution)/shard_map/all_to_all | solution.py:144
  759.5 52.8 %all-to-all-start.2 = ((bf16[32,32,1024]{2,1,0:T(8,128)(2,1)}), bf16[32,32,1024]{2,1,0:T(8,128)(2,1)}, u32[]{:S(2)}, u32[]{:S(2)}) async-start(bf16[32,32,1024]{2,1,0:T(8,128)(2,1)} %bitcast.148), calls=%async_computation.2 | async-start | bytes 4194304 | tf_op jit(solution)/shard_map/all_to_all | solution.py:86
  763.5 6.1 copy-start.8
  763.5 6.1 copy-start.21
  769.6 4.3 copy-start.16
  802.3 14.2 %copy-start.14 = (s32[1024]{0:T(1024)S(1)}, s32[1024]{0:T(1024)}, u32[]{:S(2)}) copy-start(s32[1024]{0:T(1024)} %copy-done.13) | copy-start | bytes 12292
  812.3 53.0 %all-to-all-start.4 = ((bf16[32,32,1024]{2,1,0:T(8,128)(2,1)}), bf16[32,32,1024]{2,1,0:T(8,128)(2,1)}, u32[]{:S(2)}, u32[]{:S(2)}) async-start(bf16[32,32,1024]{2,1,0:T(8,128)(2,1)} %bitcast.149), calls=%async_computation.4 | async-start | bytes 4194304 | tf_op jit(solution)/shard_map/all_to_all | solution.py:86
Sparse Core Ops, SparseCore 0:
  44.2 3.2 sort.72.cloned.1.call-done
  (1 shorter events, 0.0 us)
where the time goes:
time: 893 us; the launch traced here: 880 us
  local copies, waits for them, and re-layouts  268 us (30%)
  matrix products  241 us (27%)
  waiting for transfers between devices  176 us (20%)
  other arithmetic  140 us (16%)
  starting transfers between devices  40.9 us (5%)
  between operations  14.5 us (2%)
    all_to_all x3, waiting for transfers between devices, regroup(): lax.all_to_all(buffer, ('row', 'col'), split_axis=0, concat_axis=0, tiled...  119 us
    dot_general x2, matrix products, attend(): jnp.einsum('bhqk,bqhd->bkhd', grad_score, q_heads, preferred_element_type...  71.7 us
    dot_general x2, matrix products, attend(): jnp.einsum('bhqk,bkhd->bqhd', grad_score, k_heads, preferred_element_type...  70.4 us
    scatter-add x2, other arithmetic, per_group(): totals = totals.at[read_group.reshape(-1)].add(grad_tiles)  68.4 us
    all_to_all x1, waiting for transfers between devices, body(): lax.all_to_all(outbound, 'col', split_axis=0, concat_axis=0, tiled=True)  39.6 us
    slice x4, local copies, waits for them, and re-layouts, per_group(): picked_kv[:, :, :width]  24.2 us
    concatenate x2, other arithmetic, per_group(): jnp.concatenate([grad_key.reshape(-1, block_rows, width), grad_value.resh...  23.3 us
    all_to_all x1, starting transfers between devices, body(): lax.all_to_all(outbound, 'col', split_axis=0, concat_axis=0, tiled=True)  20.7 us
  transfers between devices with their start and end apart: 5, of which 5 were waited for; matrix products, arithmetic and copies ran while one was open for 10% of the time, Pallas kernels for 0%

commit v1 on v0

--- a/solution.py
+++ b/solution.py
@@ -5,6 +5,23 @@
 
 HEADS = 8
 HEAD_DIM = 128
+
+
+def _report_terms(message, row_dim, frame_in):
+    s_next, t_next = (message.shape[:row_dim], message.shape[row_dim + 1 :])
+    long_array = jnp.moveaxis(message.reshape(*s_next, frame_in, -1, *t_next), row_dim, 0)
+    return long_array
+
+
+def hubs_map(array_here, in_dim):
+    array_here = jnp.moveaxis(array_here, 0, in_dim)
+    outcome_arr = array_here.shape
+    parts_out = array_here.reshape(
+        *outcome_arr[:in_dim],
+        outcome_arr[in_dim] * outcome_arr[in_dim + 1],
+        *outcome_arr[in_dim + 2 :]
+    )
+    return parts_out
 
 
 def attend(queries, key_rows, value_rows, cot_rows, gain_row):
@@ -141,7 +158,16 @@
     remote_rows = remote_kv.reshape(col_count * capacity * block_rows, 2 * width)
     remote_proj = project_back(remote_rows, w_key, w_value, width).astype(jnp.bfloat16)
     remote_proj = remote_proj.reshape(col_count, capacity, block_rows * width)
-    returned = lax.all_to_all(remote_proj, "col", split_axis=0, concat_axis=0, tiled=True)
+    piece_now, piece_next = (lax.axis_size("col"), lax.axis_index("col"))
+    found_now = _report_terms(remote_proj, 0, piece_now)
+    gallery = [found_now[piece_next]]
+    for pp in range(1, piece_now):
+        small = found_now[piece_next ^ pp]
+        gallery.append(
+            lax.ppermute(small, axis_name="col", perm=[(k, k ^ pp) for k in range(piece_now)])
+        )
+    found_now = jnp.stack(gallery)[piece_next ^ jnp.arange(piece_now)]
+    returned = hubs_map(found_now, 0)
     returned = returned.reshape(col_count * capacity, block_rows * width).astype(jnp.float32)
     back_sum = lax.dot_general(
         back_hot, returned, (((0,), (0,)), ((), ())), precision=lax.Precision.HIGHEST

time: 893 us -> 889 us (level)
  local copies, waits for them, and re-layouts: 268 us -> 287 us
  waiting for transfers between devices: 176 us -> 157 us
  starting transfers between devices: 40.9 us -> 26.1 us
  other arithmetic: 140 us -> 151 us
    all_to_all x1 -> x0, waiting for transfers between devices: 17.7 us -> none  [body(): lax.all_to_all(remote_proj, 'col', split_axis=0, concat_axis=0, tiled=True)]
    all_to_all x1, starting transfers between devices: 20.7 us -> 5.13 us  [body(): lax.all_to_all(outbound, 'col', split_axis=0, concat_axis=0, tiled=True)]
    gather x0 -> x3, local copies, waits for them, and re-layouts: none -> 11.2 us  [body(): found_now = jnp.stack(gallery)[piece_next ^ jnp.arange(piece_now)]]
    ppermute x0 -> x3, waiting for transfers between devices: none -> 10.4 us  [body(): lax.ppermute(small, axis_name='col', perm=[(k, k ^ pp) for k in range(pie...]
    all_to_all x3, waiting for transfers between devices: 119 us -> 109 us  [regroup(): lax.all_to_all(buffer, ('row', 'col'), split_axis=0, concat_axis=0, tiled...]
  transfers between devices with their start and end apart: 5 -> 7, of which waited for: 5 -> 4; matrix products, arithmetic and copies ran while one was open for 10% -> 13% of each run, Pallas kernels for 0% -> 0%
where the time goes in v1:
time: 889 us; the launch traced here: 876 us
  local copies, waits for them, and re-layouts  287 us (32%)
  matrix products  240 us (27%)
  waiting for transfers between devices  157 us (18%)
  other arithmetic  151 us (17%)
  starting transfers between devices  26.1 us (3%)
  between operations  14.7 us (2%)
    all_to_all x3, waiting for transfers between devices, regroup(): lax.all_to_all(buffer, ('row', 'col'), split_axis=0, concat_axis=0, tiled...  109 us
    dot_general x2, matrix products, attend(): jnp.einsum('bhqk,bqhd->bkhd', grad_score, q_heads, preferred_element_type...  71.7 us
    dot_general x2, matrix products, attend(): jnp.einsum('bhqk,bkhd->bqhd', grad_score, k_heads, preferred_element_type...  70.4 us
    scatter-add x2, other arithmetic, per_group(): totals = totals.at[read_group.reshape(-1)].add(grad_tiles)  68.4 us
    all_to_all x1, waiting for transfers between devices, body(): lax.all_to_all(outbound, 'col', split_axis=0, concat_axis=0, tiled=True)  37.5 us
    slice x4, local copies, waits for them, and re-layouts, per_group(): picked_kv[:, :, :width]  24.2 us
    concatenate x2, other arithmetic, per_group(): jnp.concatenate([grad_key.reshape(-1, block_rows, width), grad_value.resh...  23.3 us
    transpose x2, local copies, waits for them, and re-layouts, attend(): jnp.einsum('bhqk,bqhd->bkhd', grad_score, q_heads, preferred_element_type...  19.9 us
  transfers between devices with their start and end apart: 7, of which 4 were waited for; matrix products, arithmetic and copies ran while one was open for 13% of the time, Pallas kernels for 0%

profile of v1, /device:TPU:0, one launch (start us, length us, event | category | flops | bytes accessed | tf_op | source)
XLA Modules:
  0.0 876.5 jit_solution(8850724626194814495)
XLA Ops:
  12.4 7.9 gather_fusion.1
  20.3 7.9 gather_fusion.2
  32.9 7.4 all-to-all-start
  48.5 8.6 gather_fusion.9
  62.4 72.3 %all-to-all-done = bf16[32,32,2048]{2,1,0:T(8,128)(2,1)} async-done(((bf16[32,32,2048]{2,1,0:T(8,128)(2,1)}), bf16[32,32,2048]{2,1,0:T(8,128)(2,1)}, u32[]{:S(2)}, u32[]{:S(2)}) %all-to-all-start) | async-done | bytes 4194336 | tf_op jit(solution)/shard_map/all_to_all | solution.py:103
  134.7 11.6 %gather_fusion.3 = bf16[1024,2048]{1,0:T(8,128)(2,1)} fusion(bf16[1024,2048]{1,0:T(8,128)(2,1)} %bitcast.16, s32[1024]{0:T(1024)S(1)} %fusion.61), kind=kCustom, calls=%fused_computation.3 | custom fusion | bytes 8392704 | tf_op jit(solution)/shard_map/gather | solution.py:108
  155.2 6.5 copy.54
  187.0 37.5 %all-to-all-done.1 = bf16[4,2,128,2048]{3,2,1,0:T(8,128)(2,1)} async-done(((bf16[4,2,128,2048]{3,2,1,0:T(8,128)(2,1)}), bf16[4,2,128,2048]{3,2,1,0:T(8,128)(2,1)}, u32[]{:S(2)}, u32[]{:S(2)}) %all-to-all-start.1) | async-done | bytes 4194336 | tf_op jit(solution)/shard_map/all_to_all | solution.py:123
  224.5 7.4 pad_maximum_fusion.1
  231.9 7.8 broadcast_in_dim.30
  239.8 454.8 %while.14 = (s32[]{:T(128)}, f32[16,128,2048]{2,1,0:T(8,128)}, bf16[2,4,128,1024]{3,2,1,0:T(8,128)(2,1)}, bf16[2,4,128,1024]{3,2,1,0:T(8,128)(2,1)}, s32[2,4,4]{...) while((s32[]{:T(128)}, f32[16,128,2048]{2,1,0:T(8,128)}, ...), condition=%wide.region_10.11_spmd, body=%wide.region_3.10_spmd.sunk | while | flops 3283102720 | bytes 372362752 | solution.py:152
  240.3 8.1 gather_fusion
  254.3 6.2 copy.72
  263.1 8.5 fusion.124
  271.6 6.2 copy.70
  280.4 6.5 fusion.125
  294.5 35.2 %fusion.129 = bf16[4,8,128,128]{3,2,1,0:T(8,128)(2,1)} fusion(bf16[4,512,8,128]{1,3,2,0:T(8,128)(2,1)} %bitcast.151, f32[4,8,128,512]{3,2,1,0:T(8,128)} %fusion.127, f32[4,8,128,512]{3,2,1,0:T(8,128)} %get-tuple-element.198, f32[4,8,128]{2,1,0:T(8,128)S(1)} %get-tuple-element.199), kind=kOutput, calls=%fused_computation.45.clone.1 | convolution fusion | flops 552079872 | bytes 22036480 | tf_op jit(solution)/shard_map/while/body/eval_jaxpr/bhqk,bkhd->bqhd/dot_general | solution.py:56
  339.1 35.9 %fusion.128 = f32[4,512,8,128]{1,3,2,0:T(8,128)} fusion(bf16[4,128,8,128]{1,3,2,0:T(8,128)(2,1)} %bitcast.156, f32[4,8,128,512]{3,2,1,0:T(8,128)} %fusion.127, f32[4,8,128,512]{3,2,1,0:T(8,128)} %get-tuple-element.198, f32[4,8,128]{2,1,0:T(8,128)S(1)} %get-tuple-element.199), kind=kOutput, calls=%fused_computation.26.clone.1 | convolution fusion | flops 551555584 | bytes 26230784 | tf_op jit(solution)/shard_map/while/body/eval_jaxpr/bhqk,bqhd->bkhd/dot_general | solution.py:60
  375.0 9.9 %copy.74 = f32[4,512,8,128]{3,2,1,0:T(8,128)} copy(f32[4,512,8,128]{1,3,2,0:T(8,128)} %fusion.128) | data formatting | bytes 16777216 | tf_op jit(solution)/shard_map/while/body/eval_jaxpr/bhqk,bqhd->bkhd/transpose | solution.py:60
  384.9 9.3 %reshape.440 = f32[16,128,1024]{2,1,0:T(8,128)} reshape(f32[4,512,8,128]{3,2,1,0:T(8,128)} %copy.74) | data formatting | bytes 16777216 | tf_op jit(solution)/shard_map/while/body/eval_jaxpr/reshape;while/body/eval_jaxpr/reshape | solution.py:140
  394.3 7.9 convolution_bitcast_fusion.2
  402.2 9.9 %copy.73 = f32[4,512,8,128]{3,2,1,0:T(8,128)} copy(f32[4,512,8,128]{1,3,2,0:T(8,128)} %convolution_bitcast_fusion.2) | data formatting | bytes 16777216 | tf_op jit(solution)/shard_map/while/body/eval_jaxpr/bhqk,bqhd->bkhd/transpose | solution.py:63
  412.1 9.2 %reshape.439 = f32[16,128,1024]{2,1,0:T(8,128)} reshape(f32[4,512,8,128]{3,2,1,0:T(8,128)} %copy.73) | data formatting | bytes 16777216 | tf_op jit(solution)/shard_map/while/body/eval_jaxpr/reshape;while/body/eval_jaxpr/reshape | solution.py:140
  421.3 11.7 %pad_maximum_fusion.7 = f32[16,128,2048]{2,1,0:T(8,128)} fusion(f32[16,128,1024]{2,1,0:T(8,128)} %reshape.439, f32[16,128,1024]{2,1,0:T(8,128)} %reshape.440), kind=kLoop, calls=%fused_computation.15.clone.1 | loop fusion | flops 4194304 | bytes 33554432 | tf_op jit(solution)/shard_map/while/body/eval_jaxpr/concatenate | solution.py:139
  433.1 34.2 %scatter_fusion = f32[16,128,2048]{2,1,0:T(8,128)} fusion(f32[16,128,2048]{2,1,0:T(8,128)} %get-tuple-element.216, s32[16]{0:T(128)S(1)} %fusion.122, f32[16,128,2048]{2,1,0:T(8,128)} %pad_maximum_fusion.7), kind=kCustom, calls=%fused_computation.12.clone.1 | custom fusion | flops 4194304 | bytes 50331712 | tf_op jit(solution)/shard_map/while/body/eval_jaxpr/scatter-add | solution.py:143
  467.4 8.1 gather_fusion
  490.3 8.5 fusion.124
  498.7 6.2 copy.70
  507.6 6.5 fusion.125
  521.6 35.2 %fusion.129 = bf16[4,8,128,128]{3,2,1,0:T(8,128)(2,1)} fusion(bf16[4,512,8,128]{1,3,2,0:T(8,128)(2,1)} %bitcast.151, f32[4,8,128,512]{3,2,1,0:T(8,128)} %fusion.127, f32[4,8,128,512]{3,2,1,0:T(8,128)} %get-tuple-element.198, f32[4,8,128]{2,1,0:T(8,128)S(1)} %get-tuple-element.199), kind=kOutput, calls=%fused_computation.45.clone.1 | convolution fusion | flops 552079872 | bytes 22036480 | tf_op jit(solution)/shard_map/while/body/eval_jaxpr/bhqk,bkhd->bqhd/dot_general | solution.py:56
  566.2 35.9 %fusion.128 = f32[4,512,8,128]{1,3,2,0:T(8,128)} fusion(bf16[4,128,8,128]{1,3,2,0:T(8,128)(2,1)} %bitcast.156, f32[4,8,128,512]{3,2,1,0:T(8,128)} %fusion.127, f32[4,8,128,512]{3,2,1,0:T(8,128)} %get-tuple-element.198, f32[4,8,128]{2,1,0:T(8,128)S(1)} %get-tuple-element.199), kind=kOutput, calls=%fused_computation.26.clone.1 | convolution fusion | flops 551555584 | bytes 26230784 | tf_op jit(solution)/shard_map/while/body/eval_jaxpr/bhqk,bqhd->bkhd/dot_general | solution.py:60
  602.1 9.9 %copy.74 = f32[4,512,8,128]{3,2,1,0:T(8,128)} copy(f32[4,512,8,128]{1,3,2,0:T(8,128)} %fusion.128) | data formatting | bytes 16777216 | tf_op jit(solution)/shard_map/while/body/eval_jaxpr/bhqk,bqhd->bkhd/transpose | solution.py:60
  612.1 9.3 %reshape.440 = f32[16,128,1024]{2,1,0:T(8,128)} reshape(f32[4,512,8,128]{3,2,1,0:T(8,128)} %copy.74) | data formatting | bytes 16777216 | tf_op jit(solution)/shard_map/while/body/eval_jaxpr/reshape;while/body/eval_jaxpr/reshape | solution.py:140
  621.4 7.9 convolution_bitcast_fusion.2
  629.3 9.9 %copy.73 = f32[4,512,8,128]{3,2,1,0:T(8,128)} copy(f32[4,512,8,128]{1,3,2,0:T(8,128)} %convolution_bitcast_fusion.2) | data formatting | bytes 16777216 | tf_op jit(solution)/shard_map/while/body/eval_jaxpr/bhqk,bqhd->bkhd/transpose | solution.py:63
  639.2 9.2 %reshape.439 = f32[16,128,1024]{2,1,0:T(8,128)} reshape(f32[4,512,8,128]{3,2,1,0:T(8,128)} %copy.73) | data formatting | bytes 16777216 | tf_op jit(solution)/shard_map/while/body/eval_jaxpr/reshape;while/body/eval_jaxpr/reshape | solution.py:140
  648.5 11.7 %pad_maximum_fusion.7 = f32[16,128,2048]{2,1,0:T(8,128)} fusion(f32[16,128,1024]{2,1,0:T(8,128)} %reshape.439, f32[16,128,1024]{2,1,0:T(8,128)} %reshape.440), kind=kLoop, calls=%fused_computation.15.clone.1 | loop fusion | flops 4194304 | bytes 33554432 | tf_op jit(solution)/shard_map/while/body/eval_jaxpr/concatenate | solution.py:139
  660.2 34.2 %scatter_fusion = f32[16,128,2048]{2,1,0:T(8,128)} fusion(f32[16,128,2048]{2,1,0:T(8,128)} %get-tuple-element.216, s32[16]{0:T(128)S(1)} %fusion.122, f32[16,128,2048]{2,1,0:T(8,128)} %pad_maximum_fusion.7), kind=kCustom, calls=%fused_computation.12.clone.1 | custom fusion | flops 4194304 | bytes 50331712 | tf_op jit(solution)/shard_map/while/body/eval_jaxpr/scatter-add | solution.py:143
  694.6 6.6 convert.5
  724.7 7.9 gather_fusion.5
  736.4 6.6 fusion.48
  743.0 10.4 %collective-permute-done.2 = bf16[1,2,131072]{2,1,0:T(2,128)(2,1)} collective-permute-done((bf16[1,2,131072]{2,1,0:T(2,128)(2,1)S(1)}, bf16[1,2,131072]{2,1,0:T(2,128)(2,1)}, u32[]{:S(2)}, u32[]{:S(2)}) %collective-permute-start.2) | collective-permute-done | bytes 524320 | tf_op jit(solution)/shard_map/ppermute | solution.py:167
  787.2 9.6 %add_convert_fusion = bf16[1024,1024]{1,0:T(8,128)(2,1)} fusion(f32[1024,1024]{1,0:T(8,128)} %reshape.298, f32[1024,1024]{1,0:T(8,128)} %fusion.48, f32[1024,1024]{1,0:T(8,128)} %fusion.46, bf16[1024,1024]{1,0:T(8,128)(2,1)} %bitcast.176, bf16[1024,1024]{1,0:T(8,128)(2,1)} %param.14), kind=kOutput, calls=%fused_computation.66 | convolution fusion | flops 2151677952 | bytes 18874368 | tf_op jit(solution)/shard_map/dot_general | solution.py:178
  796.8 7.9 gather_fusion.7
  804.7 7.9 all-to-all-start.3
  817.0 7.9 gather_fusion.6
  824.9 36.5 %all-to-all-done.3 = bf16[32,32,1024]{2,1,0:T(8,128)(2,1)} async-done(((bf16[32,32,1024]{2,1,0:T(8,128)(2,1)}), bf16[32,32,1024]{2,1,0:T(8,128)(2,1)}, u32[]{:S(2)}, u32[]{:S(2)}) %all-to-all-start.3) | async-done | bytes 2097184 | tf_op jit(solution)/shard_map/all_to_all | solution.py:103
  861.4 7.9 gather_fusion.8
  (152 shorter events, 185.8 us)
Async XLA Ops:
  7.2 139.1 %copy-start = (bf16[1024,1024]{1,0:T(8,128)(2,1)S(1)}, bf16[1024,1024]{1,0:T(8,128)(2,1)}, u32[]{:S(2)}) copy-start(bf16[1024,1024]{1,0:T(8,128)(2,1)} %param.16) | copy-start | bytes 6291460
  12.4 7.9 copy-start.13
  32.9 7.5 copy-start.9
  32.9 9.0 %copy-start.12 = (s32[32,4,2]{0,2,1:T(2,128)S(1)}, s32[32,4,2]{0,2,1:T(2,128)}, u32[]{:S(2)}) copy-start(s32[32,4,2]{0,2,1:T(2,128)} %param.18) | copy-start | bytes 3076
  32.9 101.8 %all-to-all-start = ((bf16[32,32,2048]{2,1,0:T(8,128)(2,1)}), bf16[32,32,2048]{2,1,0:T(8,128)(2,1)}, u32[]{:S(2)}, u32[]{:S(2)}) async-start(bf16[32,32,2048]{2,1,0:T(8,128)(2,1)} %bitcast.162), calls=%async_computation | async-start | bytes 8388608 | tf_op jit(solution)/shard_map/all_to_all | solution.py:103
  40.3 7.4 sort.70.cloned.1.call-start
  146.2 4.1 copy-start.6
  146.2 4.1 copy-start.17
  171.1 5.2 copy-start.16
  171.1 53.4 %all-to-all-start.1 = ((bf16[4,2,128,2048]{3,2,1,0:T(8,128)(2,1)}), bf16[4,2,128,2048]{3,2,1,0:T(8,128)(2,1)}, u32[]{:S(2)}, u32[]{:S(2)}) async-start(bf16[4,2,128,2048]{3,2,1,0:T(8,128)(2,1)} %broadcast_select_fusion), calls=%async_computation.1 | async-start | bytes 8388608 | tf_op jit(solution)/shard_map/all_to_all | solution.py:123
  177.7 4.0 copy-start.7
  231.9 7.8 copy-start.10
  280.4 7.9 copy-start.3
  286.9 1.4 copy-start.2
  287.0 3.1 copy-start.1
  288.9 1.0 copy-start.4
  384.9 9.3 %copy-start.5 = (bf16[4,128,8,128]{1,3,2,0:T(8,128)(2,1)S(1)}, bf16[4,128,8,128]{1,3,2,0:T(8,128)(2,1)}, u32[]{:S(2)}) copy-start(bf16[4,128,8,128]{1,3,2,0:T(8,128)(2,1)} %copy-done.4) | copy-start | bytes 3145732 | tf_op jit(solution)/shard_map/while
  507.6 7.9 copy-start.3
  514.1 1.4 copy-start.2
  514.1 3.1 copy-start.1
  516.0 1.0 copy-start.4
  612.1 9.3 %copy-start.5 = (bf16[4,128,8,128]{1,3,2,0:T(8,128)(2,1)S(1)}, bf16[4,128,8,128]{1,3,2,0:T(8,128)(2,1)}, u32[]{:S(2)}) copy-start(bf16[4,128,8,128]{1,3,2,0:T(8,128)(2,1)} %copy-done.4) | copy-start | bytes 3145732 | tf_op jit(solution)/shard_map/while
  703.7 2.4 copy-start.18
  714.3 6.0 copy-start.8
  718.4 24.5 %collective-permute-start = (bf16[1,2,131072]{2,1,0:T(2,128)(2,1)}, bf16[1,2,131072]{2,1,0:T(2,128)(2,1)}, u32[]{:S(2)}, u32[]{:S(2)}) collective-permute-start(bf16[1,2,131072]{2,1,0:T(2,128)(2,1)} %get-tuple-element.127), channel_id=1, source_target_pairs={{0,1},{1,0},{2,3},{3,2},{4,5},{5,4},{6,7},{7,6},{8,9},{9,8},{10,11... | collective-permute-start | bytes 1572872 | tf_op jit(solution)/shard_map/ppermute | solution.py:167
  718.4 24.5 %collective-permute-start.1 = (bf16[1,2,131072]{2,1,0:T(2,128)(2,1)}, bf16[1,2,131072]{2,1,0:T(2,128)(2,1)}, u32[]{:S(2)}, u32[]{:S(2)}) collective-permute-start(bf16[1,2,131072]{2,1,0:T(2,128)(2,1)} %get-tuple-element.126), channel_id=1, source_target_pairs={{0,2},{1,3},{2,0},{3,1},{4,6},{5,7},{6,4},{7,5},{8,10},{9,11},{10,... | collective-permute-start | bytes 1572872 | tf_op jit(solution)/shard_map/ppermute | solution.py:167
  719.0 34.4 %collective-permute-start.2 = (bf16[1,2,131072]{2,1,0:T(2,128)(2,1)S(1)}, bf16[1,2,131072]{2,1,0:T(2,128)(2,1)}, u32[]{:S(2)}, u32[]{:S(2)}) collective-permute-start(bf16[1,2,131072]{2,1,0:T(2,128)(2,1)S(1)} %get-tuple-element.125), channel_id=1, source_target_pairs={{0,3},{1,2},{2,1},{3,0},{4,7},{5,6},{6,5},{7,4},{8,11},{9,10},{10,... | collective-permute-start | bytes 1572872 | tf_op jit(solution)/shard_map/ppermute | solution.py:167
  720.3 4.4 copy-start.11
  732.6 72.2 %all-to-all-start.2 = ((bf16[32,32,1024]{2,1,0:T(8,128)(2,1)}), bf16[32,32,1024]{2,1,0:T(8,128)(2,1)}, u32[]{:S(2)}, u32[]{:S(2)}) async-start(bf16[32,32,1024]{2,1,0:T(8,128)(2,1)} %bitcast.164), calls=%async_computation.2 | async-start | bytes 4194304 | tf_op jit(solution)/shard_map/all_to_all | solution.py:103
  769.5 8.4 copy-start.15
  804.7 7.9 copy-start.14
  804.7 56.6 %all-to-all-start.3 = ((bf16[32,32,1024]{2,1,0:T(8,128)(2,1)}), bf16[32,32,1024]{2,1,0:T(8,128)(2,1)}, u32[]{:S(2)}, u32[]{:S(2)}) async-start(bf16[32,32,1024]{2,1,0:T(8,128)(2,1)} %bitcast.165), calls=%async_computation.3 | async-start | bytes 4194304 | tf_op jit(solution)/shard_map/all_to_all | solution.py:103
Sparse Core Ops, SparseCore 0:
  44.2 3.2 sort.72.cloned.1.call-done
  (1 shorter events, 0.0 us)
